TPU v7x, 256 devices: a whole 4x4x8 slice. The times are simulated.
256 devices in a mesh: seq: 32 (over y, x, core), chan: 8 (over z).
Axes of the slice: x: 4, y: 4, z: 8, core: 2. Of those that a mesh axis runs over, the one named last changes fastest.
Arguments:
- conv_in: bfloat16 [32, 512, 512], P(None, 'seq', 'chan'), may hold values from -4 to 4
- conv_gate: bfloat16 [32, 512, 512], P(None, 'seq', 'chan'), may hold values from -4 to 4
- long_filter: float32 [32, 512, 512], P(None, 'seq', 'chan'), may hold values from -1.1 to 1.1
- skip_gain: float32 [512], P('chan'), may hold values from 0.5 to 1.5
- queries: bfloat16 [32, 512, 1024], P(None, 'seq', 'chan'), may hold values from -40 to 40
- keys_in: bfloat16 [32, 512, 1024], P(None, 'seq', 'chan'), may hold values from -40 to 40
- w_value: bfloat16 [512, 1024], P(None, 'chan'), may hold values from -0.25 to 0.25
Outputs:
- conv_out: bfloat16 [32, 512, 512], P(None, 'seq', 'chan')
- attended: bfloat16 [32, 512, 1024], P(None, 'seq', 'chan')
All inputs are finite; a program needn't handle non-finite values.
Results may differ from a plain program's by a relative error of at most 0.015.
Values may be sent and summed in bfloat16 or wider, within the bound.
A program may use at most 64 MiB of HBM per device.

v0:
```python
import math
import jax
import jax.numpy as jnp
from jax import lax
from jax.sharding import PartitionSpec as P


def mixdot(form, left, right):
    return jnp.einsum(form, left, right, precision=lax.Precision.HIGHEST)


def channel_convolve(signal, long_filter):
    moved_sig, moved_tap = (
        lax.all_to_all(
            signal.astype(jnp.bfloat16), "seq", split_axis=2, concat_axis=1, tiled=True
        ).astype(signal.dtype),
        lax.all_to_all(
            long_filter.astype(jnp.bfloat16), "seq", split_axis=2, concat_axis=1, tiled=True
        ).astype(long_filter.dtype),
    )
    blocks = moved_sig.shape[0]
    length_q = moved_sig.shape[1]
    length_p = 2 * blocks
    total = length_p * length_q
    both = jnp.concatenate([moved_sig, moved_tap], axis=2).transpose(2, 0, 1)
    iota_p = jnp.arange(length_p, dtype=jnp.int32)
    iota_r = jnp.arange(blocks, dtype=jnp.int32)
    iota_q = jnp.arange(length_q, dtype=jnp.int32)
    ang_p = (iota_p[:, None] * iota_r[None, :] % length_p).astype(jnp.float32) * (
        2.0 * math.pi / length_p
    )
    ang_q = (iota_q[:, None] * iota_q[None, :] % length_q).astype(jnp.float32) * (
        2.0 * math.pi / length_q
    )
    ang_t = (iota_p[:, None] * iota_q[None, :] % total).astype(jnp.float32) * (
        2.0 * math.pi / total
    )
    cos_p = jnp.cos(ang_p)
    sin_p = jnp.sin(ang_p)
    cos_q = jnp.cos(ang_q)
    sin_q = jnp.sin(ang_q)
    cos_t = jnp.cos(ang_t)
    sin_t = jnp.sin(ang_t)
    first_re = mixdot("kn,cnq->ckq", cos_p, both)
    first_im = -mixdot("kn,cnq->ckq", sin_p, both)
    tw_re = first_re * cos_t + first_im * sin_t
    tw_im = first_im * cos_t - first_re * sin_t
    spec_re = mixdot("ckq,qm->ckm", tw_re, cos_q) + mixdot("ckq,qm->ckm", tw_im, sin_q)
    spec_im = mixdot("ckq,qm->ckm", tw_im, cos_q) - mixdot("ckq,qm->ckm", tw_re, sin_q)
    half_count = both.shape[0] // 2
    sig_re = spec_re[:half_count]
    sig_im = spec_im[:half_count]
    tap_re = spec_re[half_count:]
    tap_im = spec_im[half_count:]
    prod_re = sig_re * tap_re - sig_im * tap_im
    prod_im = sig_re * tap_im + sig_im * tap_re
    inner_re = mixdot("ckm,mq->ckq", prod_re, cos_q) - mixdot("ckm,mq->ckq", prod_im, sin_q)
    inner_im = mixdot("ckm,mq->ckq", prod_im, cos_q) + mixdot("ckm,mq->ckq", prod_re, sin_q)
    turned_re = inner_re * cos_t - inner_im * sin_t
    turned_im = inner_im * cos_t + inner_re * sin_t
    result = (mixdot("kn,ckq->cnq", cos_p, turned_re) - mixdot("kn,ckq->cnq", sin_p, turned_im)) * (
        1.0 / total
    )
    return lax.all_to_all(
        result.transpose(1, 2, 0).astype(jnp.bfloat16),
        "seq",
        split_axis=1,
        concat_axis=2,
        tiled=True,
    ).astype(jnp.float32)


def body(conv_in, conv_gate, long_filter, skip_gain, queries, keys_in, w_value):
    blocks, slab_rows, channels = conv_in.shape
    my_index = lax.axis_index("seq")
    tokens = blocks * slab_rows
    signal = conv_in.astype(jnp.float32)
    positions = (
        jnp.arange(blocks, dtype=jnp.int32)[:, None] * tokens
        + my_index * slab_rows
        + jnp.arange(slab_rows, dtype=jnp.int32)[None, :]
    )
    convolved = channel_convolve(signal, long_filter)
    mixed = (convolved + skip_gain * signal) * conv_gate.astype(jnp.float32)
    conv_out = mixed.astype(jnp.bfloat16)
    head_size = w_value.shape[1]
    piece = lax.all_gather(conv_out, "chan", axis=2, tiled=True)
    piece_width = piece.shape[2]
    value_sum = jnp.dot(
        piece.reshape(tokens, piece_width), w_value, preferred_element_type=jnp.float32
    )
    values = value_sum.astype(jnp.bfloat16).reshape(blocks, slab_rows, head_size)
    query_rows = queries.reshape(tokens, head_size)
    query_pos = positions.reshape(tokens)
    score_scale = 1.0 / math.sqrt(head_size)
    empty_state = (
        jnp.full((tokens,), -1e30, jnp.float32),
        jnp.zeros((tokens,), jnp.float32),
        jnp.zeros((tokens, head_size), jnp.float32),
    )
    key_piece = lax.all_gather(keys_in, "seq", axis=1, tiled=True)
    value_piece = lax.all_gather(values, "seq", axis=1, tiled=True)
    width_now = key_piece.shape[1]
    target = max(1, 1024 // blocks)
    step_size = 1
    for candidate in range(min(width_now, target), 0, -1):
        step_size = candidate
        break

    def key_step(step_index, current):
        row_best, row_total, row_accum = current
        offset = step_index * step_size
        key_block = lax.dynamic_slice_in_dim(key_piece, offset, step_size, 1).reshape(
            blocks * step_size, head_size
        )
        value_block = lax.dynamic_slice_in_dim(value_piece, offset, step_size, 1).reshape(
            blocks * step_size, head_size
        )
        key_pos = (
            jnp.arange(blocks, dtype=jnp.int32)[:, None] * tokens
            + offset
            + jnp.arange(step_size, dtype=jnp.int32)[None, :]
        ).reshape(blocks * step_size)
        scores = (
            jnp.einsum("qd,kd->qk", query_rows, key_block, preferred_element_type=jnp.float32)
            * score_scale
        )
        allowed = key_pos[None, :] <= query_pos[:, None]
        scores = jnp.where(allowed, scores, -1e30)
        new_best = jnp.maximum(row_best, jnp.max(scores, axis=1))
        factor = jnp.exp(row_best - new_best)
        weights = jnp.where(allowed, jnp.exp(scores - new_best[:, None]), 0.0)
        row_total = row_total * factor + jnp.sum(weights, axis=1)
        row_accum = row_accum * factor[:, None] + jnp.dot(
            weights.astype(jnp.bfloat16), value_block, preferred_element_type=jnp.float32
        )
        return (new_best, row_total, row_accum)

    final_best, final_total, final_accum = lax.fori_loop(
        0, width_now // step_size, key_step, empty_state
    )
    attended = (
        (final_accum / final_total[:, None])
        .astype(jnp.bfloat16)
        .reshape(blocks, slab_rows, head_size)
    )
    return (conv_out, attended)


def solution(mesh):
    return jax.shard_map(
        body,
        mesh=mesh,
        in_specs=(
            P(None, "seq", "chan"),
            P(None, "seq", "chan"),
            P(None, "seq", "chan"),
            P("chan"),
            P(None, "seq", "chan"),
            P(None, "seq", "chan"),
            P(None, "chan"),
        ),
        out_specs=(P(None, "seq", "chan"), P(None, "seq", "chan")),
        check_vma=False,
    )
```

profile of v0, /device:TPU:1, one launch (start us, length us, event | category | flops | bytes accessed | tf_op | source)
XLA Modules:
  0.0 245.0 jit_solution(10891590349229744156)
XLA Ops:
  10.0 8.6 %all-to-all-start.1 = ((bf16[32,2,512]{2,1,0:T(2,128)(2,1)}), bf16[32,2,512]{2,1,0:T(2,128)(2,1)S(1)}, u32[]{:S(2)}, u32[]{:S(2)}) async-start(bf16[32,2,512]{2,1,0:T(2,128)(2,1)} %reshape.130), calls=%async_computation.1 | async-start | bytes 131072 | tf_op jit(solution)/shard_map/all_to_all | solution.py:17
  18.6 1.2 copy.75
  20.7 5.2 %all-to-all-done.1 = bf16[32,2,512]{2,1,0:T(2,128)(2,1)S(1)} async-done(((bf16[32,2,512]{2,1,0:T(2,128)(2,1)}), bf16[32,2,512]{2,1,0:T(2,128)(2,1)S(1)}, u32[]{:S(2)}, u32[]{:S(2)}) %all-to-all-start.1) | async-done | bytes 65568 | tf_op jit(solution)/shard_map/all_to_all | solution.py:17
  26.0 3.9 %all-to-all-start = ((bf16[32,2,512]{2,1,0:T(2,128)(2,1)}), bf16[32,2,512]{2,1,0:T(2,128)(2,1)S(1)}, u32[]{:S(2)}, u32[]{:S(2)}) async-start(bf16[32,2,512]{2,1,0:T(2,128)(2,1)} %reshape.132), calls=%async_computation | async-start | bytes 131072 | tf_op jit(solution)/shard_map/all_to_all | solution.py:14
  30.7 6.6 %all-to-all-done = bf16[32,2,512]{2,1,0:T(2,128)(2,1)S(1)} async-done(((bf16[32,2,512]{2,1,0:T(2,128)(2,1)}), bf16[32,2,512]{2,1,0:T(2,128)(2,1)S(1)}, u32[]{:S(2)}, u32[]{:S(2)}) %all-to-all-start) | async-done | bytes 65568 | tf_op jit(solution)/shard_map/all_to_all | solution.py:14
  38.7 5.4 %fusion.30 = f32[4,64,512]{2,1,0:T(8,128)S(1)} fusion(f32[4,64,512]{2,1,0:T(8,128)S(1)} %convolution_bitcast_fusion, f32[4,64,512]{2,1,0:T(8,128)S(1)} %fusion.15, f32[64,512]{1,0:T(8,128)S(1)} %get-tuple-element.210, f32[64,512]{1,0:T(8,128)S(1)} %get-tuple-element.211), kind=kOutput, calls=%fused_computation.51 | convolution fusion | flops 809369600 | bytes 1835008 | tf_op jit(solution)/shard_map/ckq,qm->ckm/dot_general | solution.py:9
  44.1 5.4 %fusion.32 = f32[4,64,512]{2,1,0:T(8,128)S(1)} fusion(f32[4,64,512]{2,1,0:T(8,128)S(1)} %fusion.15, f32[4,64,512]{2,1,0:T(8,128)S(1)} %convolution_bitcast_fusion, f32[64,512]{1,0:T(8,128)S(1)} %get-tuple-element.210, f32[64,512]{1,0:T(8,128)S(1)} %get-tuple-element.211), kind=kOutput, calls=%fused_computation.53 | convolution fusion | flops 809369600 | bytes 1835008 | tf_op jit(solution)/shard_map/ckq,qm->ckm/dot_general | solution.py:9
  49.5 5.4 %convolution_subtract_fusion = f32[4,64,512]{2,1,0:T(8,128)S(1)} fusion(f32[4,64,512]{2,1,0:T(8,128)S(1)} %fusion.30, f32[4,64,512]{2,1,0:T(8,128)S(1)} %fusion.15, f32[4,64,512]{2,1,0:T(8,128)S(1)} %convolution_bitcast_fusion, f32[64,512]{1,0:T(8,128)S(1)} %get-tuple-element.210, f32[64,512]{1,0:T(8,128)S(1)} %get-tuple-element.211), kind=kOutput, calls=%fused_computation.28 | convolution fusion | flops 809500672 | bytes 2359296 | tf_op jit(solution)/shard_map/ckq,qm->ckm/dot_general | solution.py:9
  54.9 5.6 %convolution_add_fusion.1 = f32[4,64,512]{2,1,0:T(8,128)S(1)} fusion(f32[4,64,512]{2,1,0:T(8,128)S(1)} %fusion.32, f32[4,64,512]{2,1,0:T(8,128)S(1)} %convolution_bitcast_fusion, f32[4,64,512]{2,1,0:T(8,128)S(1)} %fusion.15, f32[64,512]{1,0:T(8,128)S(1)} %get-tuple-element.210, f32[64,512]{1,0:T(8,128)S(1)} %get-tuple-element.211), kind=kOutput, calls=%fused_computation.29 | convolution fusion | flops 809500672 | bytes 2359296 | tf_op jit(solution)/shard_map/ckq,qm->ckm/dot_general | solution.py:9
  60.6 4.9 %fusion.28 = f32[2,64,512]{2,1,0:T(8,128)S(1)} fusion(f32[2,64,512]{2,1,0:T(8,128)S(1)} %get-tuple-element.208), kind=kOutput, calls=%fused_computation.49 | convolution fusion | flops 406323200 | bytes 524288 | tf_op jit(solution)/shard_map/ckm,mq->ckq/dot_general | solution.py:9
  65.5 4.9 %fusion.26 = f32[2,64,512]{2,1,0:T(8,128)S(1)} fusion(f32[2,64,512]{2,1,0:T(8,128)S(1)} %get-tuple-element.209), kind=kOutput, calls=%fused_computation.47 | convolution fusion | flops 406323200 | bytes 524288 | tf_op jit(solution)/shard_map/ckm,mq->ckq/dot_general | solution.py:9
  70.4 4.9 %convolution_subtract_fusion.1 = f32[2,64,512]{2,1,0:T(8,128)S(1)} fusion(f32[2,64,512]{2,1,0:T(8,128)S(1)} %fusion.28, f32[2,64,512]{2,1,0:T(8,128)S(1)} %get-tuple-element.209), kind=kOutput, calls=%fused_computation.34 | convolution fusion | flops 406388736 | bytes 786432 | tf_op jit(solution)/shard_map/ckm,mq->ckq/dot_general | solution.py:9
  75.2 5.1 %convolution_add_fusion.2 = f32[2,64,512]{2,1,0:T(8,128)S(1)} fusion(f32[2,64,512]{2,1,0:T(8,128)S(1)} %fusion.26, f32[2,64,512]{2,1,0:T(8,128)S(1)} %get-tuple-element.208), kind=kOutput, calls=%fused_computation.33 | convolution fusion | flops 406388736 | bytes 786432 | tf_op jit(solution)/shard_map/ckm,mq->ckq/dot_general | solution.py:9
  82.2 3.9 %all-to-all-start.2 = ((bf16[32,2,512]{2,1,0:T(2,128)(2,1)}), bf16[32,2,512]{2,1,0:T(2,128)(2,1)S(1)}, u32[]{:S(2)}, u32[]{:S(2)}) async-start(bf16[32,2,512]{2,1,0:T(2,128)(2,1)} %reshape.134), calls=%async_computation.2 | async-start | bytes 131072 | tf_op jit(solution)/shard_map/all_to_all | solution.py:64
  86.5 7.1 %all-to-all-done.2 = bf16[32,2,512]{2,1,0:T(2,128)(2,1)S(1)} async-done(((bf16[32,2,512]{2,1,0:T(2,128)(2,1)}), bf16[32,2,512]{2,1,0:T(2,128)(2,1)S(1)}, u32[]{:S(2)}, u32[]{:S(2)}) %all-to-all-start.2) | async-done | bytes 65568 | tf_op jit(solution)/shard_map/all_to_all | solution.py:64
  94.1 28.8 %all_gather.10 = bf16[32,16,512]{0,1,2:T(8,128)(2,1)S(1)} all-gather(bf16[32,16,64]{0,1,2:T(8,128)(2,1)S(1)} %fusion.38), channel_id=1, replica_groups=mesh['seq'=32,'chan'=8] {'chan'}, dimensions={2}, use_global_device_ids=true | all-gather | bytes 589824 | tf_op jit(solution)/shard_map/all_gather | solution.py:87
  123.0 2.2 copy.86
  127.2 53.7 %all-gather.5.cloned.1.call-done = bf16[32,512,128]{2,1,0:T(8,128)(2,1)} async-done(((bf16[32,16,128]{2,1,0:T(8,128)(2,1)}), bf16[32,512,128]{2,1,0:T(8,128)(2,1)}) %all-gather.5.cloned.1.call-update) | async-done | bytes 4194320 | tf_op jit(solution)/shard_map/all_gather | solution.py:102
  180.8 56.5 %while.18 = (s32[]{:T(128)}, f32[512]{0:T(512)S(1)}, f32[512]{0:T(512)S(1)}, f32[512,128]{1,0:T(8,128)S(1)}, bf16[32,512,128]{2,1,0:T(8,128)(2,1)}, /*index=5*/b...) while((s32[]{:T(128)}, f32[512]{0:T(512)S(1)}, ...), condition=%wide.region_3.4_spmd.clone, body=%wide.region_0.3_spmd.clone.sunk | while | flops 277024832 | bytes 8589887 | solution.py:139
  181.1 1.1 constant_dynamic-slice_fusion.3
  184.7 1.1 constant_dynamic-slice_fusion.3
  188.2 1.1 constant_dynamic-slice_fusion.3
  191.7 1.1 constant_dynamic-slice_fusion.3
  195.3 1.1 constant_dynamic-slice_fusion.3
  198.8 1.1 constant_dynamic-slice_fusion.3
  202.3 1.1 constant_dynamic-slice_fusion.3
  205.9 1.1 constant_dynamic-slice_fusion.3
  209.4 1.1 constant_dynamic-slice_fusion.3
  212.9 1.1 constant_dynamic-slice_fusion.3
  216.4 1.1 constant_dynamic-slice_fusion.3
  223.5 1.1 constant_dynamic-slice_fusion.3
  234.1 1.1 constant_dynamic-slice_fusion.3
  (223 shorter events, 52.9 us)
Async XLA Ops:
  7.2 118.0 %copy-start = (bf16[512,128]{1,0:T(8,128)(2,1)S(1)}, bf16[512,128]{1,0:T(8,128)(2,1)}, u32[]{:S(2)}) copy-start(bf16[512,128]{1,0:T(8,128)(2,1)} %param.15) | copy-start | bytes 393220
  7.2 120.0 %all-gather.3.cloned.1.call-start = ((), (), s32[]{:S(2)}) async-start(), calls=%async_computation.3 | async-start | bytes 4325376 | tf_op jit(solution)/shard_map/all_gather | solution.py:101
  10.0 15.9 %all-to-all-start.1 = ((bf16[32,2,512]{2,1,0:T(2,128)(2,1)}), bf16[32,2,512]{2,1,0:T(2,128)(2,1)S(1)}, u32[]{:S(2)}, u32[]{:S(2)}) async-start(bf16[32,2,512]{2,1,0:T(2,128)(2,1)} %reshape.130), calls=%async_computation.1 | async-start | bytes 131072 | tf_op jit(solution)/shard_map/all_to_all | solution.py:17
  26.0 11.3 %all-to-all-start = ((bf16[32,2,512]{2,1,0:T(2,128)(2,1)}), bf16[32,2,512]{2,1,0:T(2,128)(2,1)S(1)}, u32[]{:S(2)}, u32[]{:S(2)}) async-start(bf16[32,2,512]{2,1,0:T(2,128)(2,1)} %reshape.132), calls=%async_computation | async-start | bytes 131072 | tf_op jit(solution)/shard_map/all_to_all | solution.py:14
  80.3 5.9 %copy-start.1 = (bf16[32,16,64]{2,1,0:T(8,128)(2,1)S(1)}, bf16[32,16,64]{2,1,0:T(8,128)(2,1)}, u32[]{:S(2)}) copy-start(bf16[32,16,64]{2,1,0:T(8,128)(2,1)} %param.10) | copy-start | bytes 196612
  81.2 12.8 %copy-start.2 = (f32[64]{0:T(128)S(1)}, f32[64]{0:T(128)}, u32[]{:S(2)}) copy-start(f32[64]{0:T(128)} %param.12) | copy-start | bytes 772
  82.2 11.4 %all-to-all-start.2 = ((bf16[32,2,512]{2,1,0:T(2,128)(2,1)}), bf16[32,2,512]{2,1,0:T(2,128)(2,1)S(1)}, u32[]{:S(2)}, u32[]{:S(2)}) async-start(bf16[32,2,512]{2,1,0:T(2,128)(2,1)} %reshape.134), calls=%async_computation.2 | async-start | bytes 131072 | tf_op jit(solution)/shard_map/all_to_all | solution.py:64
  86.2 94.6 %all-gather.5.cloned.1.call-start = ((), (), s32[]{:S(2)}) async-start(), calls=%async_computation.4 | async-start | bytes 4325376 | tf_op jit(solution)/shard_map/all_gather | solution.py:102
  123.0 57.8 %copy-start.3 = (bf16[32,16,128]{2,1,0:T(8,128)(2,1)S(1)}, bf16[32,16,128]{2,1,0:T(8,128)(2,1)}, u32[]{:S(2)}) copy-start(bf16[32,16,128]{2,1,0:T(8,128)(2,1)} %param.13) | copy-start | bytes 393220
Sparse Core Ops, SparseCore 0:
  10.5 58.7 all-gather.2
  126.3 54.5 all-gather.4
where the time goes:
time: 246 us; the launch traced here: 245 us
  waiting for transfers between devices  73.2 us (30%)
  matrix products  67.3 us (27%)
  blocking collectives  28.8 us (12%)
  local copies, waits for them, and re-layouts  28.4 us (12%)
  starting transfers between devices  16.5 us (7%)
  other arithmetic  15.3 us (6%)
  between operations  14.4 us (6%)
    all_gather x1, waiting for transfers between devices, body(): value_piece = lax.all_gather(values, 'seq', axis=1, tiled=True)  53.7 us
    dot_general x12, matrix products, mixdot(): return jnp.einsum(form, left, right, precision=lax.Precision.HIGHEST)  43.3 us
    all_gather x1, blocking collectives, body(): piece = lax.all_gather(conv_out, 'chan', axis=2, tiled=True)  28.8 us
    dynamic_slice x16, local copies, waits for them, and re-layouts, key_step(): lax.dynamic_slice_in_dim(value_piece, offset, step_size, 1)  17.2 us
    dot_general x16, matrix products, key_step(): jnp.dot(weights.astype(jnp.bfloat16), value_block, preferred_element_type...  15.7 us
    reduce_sum x16, other arithmetic, key_step(): row_total = row_total * factor + jnp.sum(weights, axis=1)  9.97 us
    all_to_all x1, starting transfers between devices, channel_convolve(): lax.all_to_all(long_filter.astype(jnp.bfloat16), 'seq', split_axis=2, con...  8.59 us
    dot_general x16, matrix products, key_step(): jnp.einsum('qd,kd->qk', query_rows, key_block, preferred_element_type=jnp...  7.38 us
  transfers between devices with their start and end apart: 5, of which 4 were waited for; matrix products, arithmetic and copies ran while one was open for 22% of the time, Pallas kernels for 0%

commit v1 on v0

--- a/solution.py
+++ b/solution.py
@@ -99,7 +99,8 @@
         jnp.zeros((tokens, head_size), jnp.float32),
     )
     key_piece = lax.all_gather(keys_in, "seq", axis=1, tiled=True)
-    value_piece = lax.all_gather(values, "seq", axis=1, tiled=True)
+    copies = jnp.concatenate([values] * lax.axis_size("seq"), axis=1)
+    value_piece = lax.all_to_all(copies, "seq", 1, 1, tiled=True)
     width_now = key_piece.shape[1]
     target = max(1, 1024 // blocks)
     step_size = 1

time: 246 us -> 290 us (1.18)
  local copies, waits for them, and re-layouts: 28.4 us -> 66.1 us
  starting transfers between devices: 16.5 us -> 25.8 us
  waiting for transfers between devices: 73.2 us -> 68.2 us
    all_gather x1 -> x0, waiting for transfers between devices: 53.7 us -> none  [body(): value_piece = lax.all_gather(values, 'seq', axis=1, tiled=True)]
    all_to_all x0 -> x1, waiting for transfers between devices: none -> 49.4 us  [body(): value_piece = lax.all_to_all(copies, 'seq', 1, 1, tiled=True)]
    unnamed x17 -> x48, local copies, waits for them, and re-layouts: 5.61 us -> 27 us
    dynamic_slice x0 -> x16, local copies, waits for them, and re-layouts: none -> 15.7 us  [key_step(): lax.dynamic_slice_in_dim(key_piece, offset, step_size, 1)]
    all_to_all x0 -> x1, starting transfers between devices: none -> 9.33 us  [body(): value_piece = lax.all_to_all(copies, 'seq', 1, 1, tiled=True)]
    all_to_all x1, starting transfers between devices: 3.9 us -> 8.59 us  [channel_convolve(): lax.all_to_all(signal.astype(jnp.bfloat16), 'seq', split_axis=2, concat_a...]
    all_to_all x1, starting transfers between devices: 8.59 us -> 3.9 us  [channel_convolve(): lax.all_to_all(long_filter.astype(jnp.bfloat16), 'seq', split_axis=2, con...]
    dynamic_slice x16 -> x32, local copies, waits for them, and re-layouts: 17.2 us -> 17.3 us  [key_step(): lax.dynamic_slice_in_dim(value_piece, offset, step_size, 1)]
  transfers between devices with their start and end apart: 5 -> 5, of which waited for: 4 -> 4; matrix products, arithmetic and copies ran while one was open for 22% -> 10% of each run, Pallas kernels for 0% -> 0%
where the time goes in v1:
time: 290 us; the launch traced here: 287 us
  waiting for transfers between devices  68.2 us (24%)
  matrix products  66.7 us (23%)
  local copies, waits for them, and re-layouts  66.1 us (23%)
  blocking collectives  29.2 us (10%)
  starting transfers between devices  25.8 us (9%)
  other arithmetic  15.3 us (5%)
  between operations  14.4 us (5%)
    all_to_all x1, waiting for transfers between devices, body(): value_piece = lax.all_to_all(copies, 'seq', 1, 1, tiled=True)  49.4 us
    dot_general x12, matrix products, mixdot(): return jnp.einsum(form, left, right, precision=lax.Precision.HIGHEST)  43.3 us
    all_gather x1, blocking collectives, body(): piece = lax.all_gather(conv_out, 'chan', axis=2, tiled=True)  29.2 us
    unnamed x48, local copies, waits for them, and re-layouts  27 us
    dynamic_slice x32, local copies, waits for them, and re-layouts, key_step(): lax.dynamic_slice_in_dim(value_piece, offset, step_size, 1)  17.3 us
    dynamic_slice x16, local copies, waits for them, and re-layouts, key_step(): lax.dynamic_slice_in_dim(key_piece, offset, step_size, 1)  15.7 us
    dot_general x16, matrix products, key_step(): jnp.dot(weights.astype(jnp.bfloat16), value_block, preferred_element_type...  15.6 us
    reduce_sum x16, other arithmetic, key_step(): row_total = row_total * factor + jnp.sum(weights, axis=1)  9.95 us
  transfers between devices with their start and end apart: 5, of which 4 were waited for; matrix products, arithmetic and copies ran while one was open for 10% of the time, Pallas kernels for 0%

profile of v1, /device:TPU:1, one launch (start us, length us, event | category | flops | bytes accessed | tf_op | source)
XLA Modules:
  0.0 286.9 jit_solution(2714387805621647393)
XLA Ops:
  7.2 1.2 copy.174
  9.3 8.6 %all-to-all-start = ((bf16[32,2,512]{2,1,0:T(2,128)(2,1)}), bf16[32,2,512]{2,1,0:T(2,128)(2,1)S(1)}, u32[]{:S(2)}, u32[]{:S(2)}) async-start(bf16[32,2,512]{2,1,0:T(2,128)(2,1)} %reshape.132), calls=%async_computation | async-start | bytes 131072 | tf_op jit(solution)/shard_map/all_to_all | solution.py:14
  20.0 5.2 %all-to-all-done = bf16[32,2,512]{2,1,0:T(2,128)(2,1)S(1)} async-done(((bf16[32,2,512]{2,1,0:T(2,128)(2,1)}), bf16[32,2,512]{2,1,0:T(2,128)(2,1)S(1)}, u32[]{:S(2)}, u32[]{:S(2)}) %all-to-all-start) | async-done | bytes 65568 | tf_op jit(solution)/shard_map/all_to_all | solution.py:14
  25.2 3.9 %all-to-all-start.1 = ((bf16[32,2,512]{2,1,0:T(2,128)(2,1)}), bf16[32,2,512]{2,1,0:T(2,128)(2,1)S(1)}, u32[]{:S(2)}, u32[]{:S(2)}) async-start(bf16[32,2,512]{2,1,0:T(2,128)(2,1)} %reshape.130), calls=%async_computation.1 | async-start | bytes 131072 | tf_op jit(solution)/shard_map/all_to_all | solution.py:17
  30.0 6.6 %all-to-all-done.1 = bf16[32,2,512]{2,1,0:T(2,128)(2,1)S(1)} async-done(((bf16[32,2,512]{2,1,0:T(2,128)(2,1)}), bf16[32,2,512]{2,1,0:T(2,128)(2,1)S(1)}, u32[]{:S(2)}, u32[]{:S(2)}) %all-to-all-start.1) | async-done | bytes 65568 | tf_op jit(solution)/shard_map/all_to_all | solution.py:17
  37.9 5.4 %fusion.32 = f32[4,64,512]{2,1,0:T(8,128)S(1)} fusion(f32[4,64,512]{2,1,0:T(8,128)S(1)} %fusion.15, f32[4,64,512]{2,1,0:T(8,128)S(1)} %convolution_bitcast_fusion, f32[64,512]{1,0:T(8,128)S(1)} %get-tuple-element.240, f32[64,512]{1,0:T(8,128)S(1)} %get-tuple-element.241), kind=kOutput, calls=%fused_computation.53 | convolution fusion | flops 809369600 | bytes 1835008 | tf_op jit(solution)/shard_map/ckq,qm->ckm/dot_general | solution.py:9
  43.3 5.4 %fusion.30 = f32[4,64,512]{2,1,0:T(8,128)S(1)} fusion(f32[4,64,512]{2,1,0:T(8,128)S(1)} %convolution_bitcast_fusion, f32[4,64,512]{2,1,0:T(8,128)S(1)} %fusion.15, f32[64,512]{1,0:T(8,128)S(1)} %get-tuple-element.240, f32[64,512]{1,0:T(8,128)S(1)} %get-tuple-element.241), kind=kOutput, calls=%fused_computation.51 | convolution fusion | flops 809369600 | bytes 1835008 | tf_op jit(solution)/shard_map/ckq,qm->ckm/dot_general | solution.py:9
  48.8 5.4 %convolution_add_fusion.1 = f32[4,64,512]{2,1,0:T(8,128)S(1)} fusion(f32[4,64,512]{2,1,0:T(8,128)S(1)} %fusion.32, f32[4,64,512]{2,1,0:T(8,128)S(1)} %convolution_bitcast_fusion, f32[4,64,512]{2,1,0:T(8,128)S(1)} %fusion.15, f32[64,512]{1,0:T(8,128)S(1)} %get-tuple-element.240, f32[64,512]{1,0:T(8,128)S(1)} %get-tuple-element.241), kind=kOutput, calls=%fused_computation.29 | convolution fusion | flops 809500672 | bytes 2359296 | tf_op jit(solution)/shard_map/ckq,qm->ckm/dot_general | solution.py:9
  54.2 5.6 %convolution_subtract_fusion = f32[4,64,512]{2,1,0:T(8,128)S(1)} fusion(f32[4,64,512]{2,1,0:T(8,128)S(1)} %fusion.30, f32[4,64,512]{2,1,0:T(8,128)S(1)} %fusion.15, f32[4,64,512]{2,1,0:T(8,128)S(1)} %convolution_bitcast_fusion, f32[64,512]{1,0:T(8,128)S(1)} %get-tuple-element.240, f32[64,512]{1,0:T(8,128)S(1)} %get-tuple-element.241), kind=kOutput, calls=%fused_computation.28 | convolution fusion | flops 809500672 | bytes 2359296 | tf_op jit(solution)/shard_map/ckq,qm->ckm/dot_general | solution.py:9
  59.9 4.9 %fusion.28 = f32[2,64,512]{2,1,0:T(8,128)S(1)} fusion(f32[2,64,512]{2,1,0:T(8,128)S(1)} %get-tuple-element.238), kind=kOutput, calls=%fused_computation.49 | convolution fusion | flops 406323200 | bytes 524288 | tf_op jit(solution)/shard_map/ckm,mq->ckq/dot_general | solution.py:9
  64.8 4.9 %fusion.26 = f32[2,64,512]{2,1,0:T(8,128)S(1)} fusion(f32[2,64,512]{2,1,0:T(8,128)S(1)} %get-tuple-element.239), kind=kOutput, calls=%fused_computation.47 | convolution fusion | flops 406323200 | bytes 524288 | tf_op jit(solution)/shard_map/ckm,mq->ckq/dot_general | solution.py:9
  69.6 4.9 %convolution_subtract_fusion.1 = f32[2,64,512]{2,1,0:T(8,128)S(1)} fusion(f32[2,64,512]{2,1,0:T(8,128)S(1)} %fusion.28, f32[2,64,512]{2,1,0:T(8,128)S(1)} %get-tuple-element.239), kind=kOutput, calls=%fused_computation.34 | convolution fusion | flops 406388736 | bytes 786432 | tf_op jit(solution)/shard_map/ckm,mq->ckq/dot_general | solution.py:9
  74.5 5.1 %convolution_add_fusion.2 = f32[2,64,512]{2,1,0:T(8,128)S(1)} fusion(f32[2,64,512]{2,1,0:T(8,128)S(1)} %fusion.26, f32[2,64,512]{2,1,0:T(8,128)S(1)} %get-tuple-element.238), kind=kOutput, calls=%fused_computation.33 | convolution fusion | flops 406388736 | bytes 786432 | tf_op jit(solution)/shard_map/ckm,mq->ckq/dot_general | solution.py:9
  81.5 3.9 %all-to-all-start.2 = ((bf16[32,2,512]{2,1,0:T(2,128)(2,1)}), bf16[32,2,512]{2,1,0:T(2,128)(2,1)S(1)}, u32[]{:S(2)}, u32[]{:S(2)}) async-start(bf16[32,2,512]{2,1,0:T(2,128)(2,1)} %reshape.134), calls=%async_computation.2 | async-start | bytes 131072 | tf_op jit(solution)/shard_map/all_to_all | solution.py:64
  86.4 6.4 %all-to-all-done.2 = bf16[32,2,512]{2,1,0:T(2,128)(2,1)S(1)} async-done(((bf16[32,2,512]{2,1,0:T(2,128)(2,1)}), bf16[32,2,512]{2,1,0:T(2,128)(2,1)S(1)}, u32[]{:S(2)}, u32[]{:S(2)}) %all-to-all-start.2) | async-done | bytes 65568 | tf_op jit(solution)/shard_map/all_to_all | solution.py:64
  93.4 29.2 %all_gather.7 = bf16[32,16,512]{0,1,2:T(8,128)(2,1)S(1)} all-gather(bf16[32,16,64]{0,1,2:T(8,128)(2,1)S(1)} %fusion.38), channel_id=1, replica_groups=mesh['seq'=32,'chan'=8] {'chan'}, dimensions={2}, use_global_device_ids=true | all-gather | bytes 589824 | tf_op jit(solution)/shard_map/all_gather | solution.py:87
  122.6 2.2 copy.185
  147.1 9.3 %all-to-all-start.3 = ((bf16[32,512,128]{2,0,1:T(8,128)(2,1)}), bf16[32,512,128]{2,0,1:T(8,128)(2,1)}, u32[]{:S(2)}, u32[]{:S(2)}) async-start(bf16[32,512,128]{2,0,1:T(8,128)(2,1)} %constant_dynamic-update-slice_fusion), calls=%async_computation.3 | async-start | bytes 8388608 | tf_op jit(solution)/shard_map/all_to_all | solution.py:103
  157.5 49.4 %all-to-all-done.3 = bf16[32,512,128]{2,0,1:T(8,128)(2,1)} async-done(((bf16[32,512,128]{2,0,1:T(8,128)(2,1)}), bf16[32,512,128]{2,0,1:T(8,128)(2,1)}, u32[]{:S(2)}, u32[]{:S(2)}) %all-to-all-start.3) | async-done | bytes 4194336 | tf_op jit(solution)/shard_map/all_to_all | solution.py:103
  206.9 72.4 %while.18 = (s32[]{:T(128)}, f32[512]{0:T(512)S(1)}, f32[512]{0:T(512)S(1)}, f32[512,128]{1,0:T(8,128)S(1)}, bf16[32,512,128]{2,1,0:T(8,128)(2,1)}, /*index=5*/b...) while((s32[]{:T(128)}, f32[512]{0:T(512)S(1)}, ...), condition=%wide.region_3.4_spmd.clone, body=%wide.region_0.3_spmd.clone.sunk | while | flops 277024832 | bytes 9114171 | solution.py:140
  211.4 1.0 constant_dynamic-slice_fusion.4
  215.9 1.0 constant_dynamic-slice_fusion.4
  220.4 1.0 constant_dynamic-slice_fusion.4
  225.0 1.0 constant_dynamic-slice_fusion.4
  229.5 1.0 constant_dynamic-slice_fusion.4
  234.0 1.0 constant_dynamic-slice_fusion.4
  238.5 1.0 constant_dynamic-slice_fusion.4
  243.1 1.0 constant_dynamic-slice_fusion.4
  247.6 1.0 constant_dynamic-slice_fusion.4
  252.1 1.0 constant_dynamic-slice_fusion.4
  256.7 1.0 constant_dynamic-slice_fusion.4
  261.2 1.0 constant_dynamic-slice_fusion.4
  (286 shorter events, 92.2 us)
Async XLA Ops:
  7.2 117.6 %copy-start = (bf16[512,128]{1,0:T(8,128)(2,1)S(1)}, bf16[512,128]{1,0:T(8,128)(2,1)}, u32[]{:S(2)}) copy-start(bf16[512,128]{1,0:T(8,128)(2,1)} %param.15) | copy-start | bytes 393220
  9.3 15.9 %all-to-all-start = ((bf16[32,2,512]{2,1,0:T(2,128)(2,1)}), bf16[32,2,512]{2,1,0:T(2,128)(2,1)S(1)}, u32[]{:S(2)}, u32[]{:S(2)}) async-start(bf16[32,2,512]{2,1,0:T(2,128)(2,1)} %reshape.132), calls=%async_computation | async-start | bytes 131072 | tf_op jit(solution)/shard_map/all_to_all | solution.py:14
  25.2 11.3 %all-to-all-start.1 = ((bf16[32,2,512]{2,1,0:T(2,128)(2,1)}), bf16[32,2,512]{2,1,0:T(2,128)(2,1)S(1)}, u32[]{:S(2)}, u32[]{:S(2)}) async-start(bf16[32,2,512]{2,1,0:T(2,128)(2,1)} %reshape.130), calls=%async_computation.1 | async-start | bytes 131072 | tf_op jit(solution)/shard_map/all_to_all | solution.py:17
  74.5 11.6 %copy-start.1 = (bf16[32,16,64]{2,1,0:T(8,128)(2,1)S(1)}, bf16[32,16,64]{2,1,0:T(8,128)(2,1)}, u32[]{:S(2)}) copy-start(bf16[32,16,64]{2,1,0:T(8,128)(2,1)} %param.10) | copy-start | bytes 196612
  74.5 18.7 %copy-start.2 = (f32[64]{0:T(128)S(1)}, f32[64]{0:T(128)}, u32[]{:S(2)}) copy-start(f32[64]{0:T(128)} %param.12) | copy-start | bytes 772
  81.5 11.3 %all-to-all-start.2 = ((bf16[32,2,512]{2,1,0:T(2,128)(2,1)}), bf16[32,2,512]{2,1,0:T(2,128)(2,1)S(1)}, u32[]{:S(2)}, u32[]{:S(2)}) async-start(bf16[32,2,512]{2,1,0:T(2,128)(2,1)} %reshape.134), calls=%async_computation.2 | async-start | bytes 131072 | tf_op jit(solution)/shard_map/all_to_all | solution.py:64
  85.4 121.4 %all-gather.2.cloned.1.call-start = ((), (), s32[]{:S(2)}) async-start(), calls=%async_computation.4 | async-start | bytes 4325376 | tf_op jit(solution)/shard_map/all_gather | solution.py:101
  147.1 59.7 %copy-start.3 = (bf16[32,16,128]{2,1,0:T(8,128)(2,1)S(1)}, bf16[32,16,128]{2,1,0:T(8,128)(2,1)}, u32[]{:S(2)}) copy-start(bf16[32,16,128]{2,1,0:T(8,128)(2,1)} %param.13) | copy-start | bytes 393220
  147.1 59.7 %all-to-all-start.3 = ((bf16[32,512,128]{2,0,1:T(8,128)(2,1)}), bf16[32,512,128]{2,0,1:T(8,128)(2,1)}, u32[]{:S(2)}, u32[]{:S(2)}) async-start(bf16[32,512,128]{2,0,1:T(8,128)(2,1)} %constant_dynamic-update-slice_fusion), calls=%async_computation.3 | async-start | bytes 8388608 | tf_op jit(solution)/shard_map/all_to_all | solution.py:103
Sparse Core Ops, SparseCore 0:
  88.7 57.3 all-gather.1
